TPU v7x, 128 devices: a whole 4x4x4 slice. The times are simulated.
128 devices in a mesh: tgt: 8 (over y_hi, x), src: 16 (over y_lo, z, core).
Axes of the slice: x: 4, y: 4 (y_hi: 2, y_lo: 2; y = y_hi * 2 + y_lo), z: 4, core: 2. Of those that a mesh axis runs over, the one named last changes fastest.
Arguments:
- positions: float32 [3, 32768], P(None, ('tgt', 'src')), may hold values from -6 to 6
- forces: float32 [3, 32768], P(None, ('tgt', 'src')), may hold values from -6 to 6
- neighbours: int32 [12, 32768], P(None, ('tgt', 'src')), may hold values from 0 to 255
- patch_owner: int32 [32768, 1], P(('tgt', 'src')), may hold values from 0 to 127; in each aligned block of 256 rows (0 to 255, 256 to 511, ...) at most 10 rows name the same one
- rest_length: float32 [6, 163840], P(None, ('tgt', 'src')), may hold values from 1 to 4
- moduli: float32 [2, 163840], P(None, ('tgt', 'src')), may hold values from 0.1 to 1
- rest_bend: float32 [3, 163840], P(None, ('tgt', 'src')), may hold values from -3 to 3
Outputs:
- final_positions: float32 [3, 32768], P(None, ('tgt', 'src'))
- final_velocity: float32 [3, 32768], P(None, ('tgt', 'src'))
Inputs may be any that keep to these rules, and one draw needn't show every extreme that they name: patch_owner[n, 0] is a flattened device index, tgt slowest; within the 256 nodes of one device no owner is named more than 10 times, and some device names some owner exactly 10 times. `neighbours`: indices into the node's own block of 256 nodes.
All inputs are finite; a program needn't handle non-finite values.
Results may differ from a plain program's by a relative error of at most 0.0003.
Values sent between devices are 32-bit elements; how exact they have to be, the bound alone decides.
A program may use at most 64 MiB of HBM per device.

v0:
```python
import math

import jax
import jax.numpy as jnp
from jax import lax
from jax.sharding import PartitionSpec as P

STEPS = 3


blob_square = 0.0025
time_step = 0.5


def stokes_block(target_pos, source_pos, source_force):
    delta = target_pos[:, :, None] - source_pos[:, None, :]
    radius_sq = jnp.sum(delta * delta, axis=0)
    shifted = radius_sq + blob_square
    inverse = 1.0 / (shifted * jnp.sqrt(shifted))
    along = jnp.sum(delta * source_force[:, None, :], axis=0)
    direct = (radius_sq + 2.0 * blob_square) * inverse
    tensor = along * inverse
    return jnp.sum(direct[None] * source_force[:, None, :] + tensor[None] * delta, axis=2)


def stokes_sum(target_pos, source_pos, source_force):
    count_target = target_pos.shape[1]
    count_source = source_pos.shape[1]
    target_rows = 512
    source_rows = 2048
    targets = target_pos.reshape(3, count_target // target_rows, target_rows).transpose(1, 0, 2)
    sources = source_pos.reshape(3, count_source // source_rows, source_rows).transpose(1, 0, 2)
    weights = source_force.reshape(3, count_source // source_rows, source_rows).transpose(1, 0, 2)

    def per_target(target_block):

        def add_block(running, blocks):
            return (running + stokes_block(target_block, blocks[0], blocks[1]), None)

        total, _ = lax.scan(add_block, jnp.zeros((3, target_rows), jnp.float32), (sources, weights))
        return total

    result = lax.map(per_target, targets)
    return result.transpose(1, 0, 2).reshape(3, count_target)


def cycle_weights():
    return jnp.concatenate(
        [jnp.full((6,), 2.0 / 9.0, jnp.float32), jnp.full((6,), -1.0 / 18.0, jnp.float32)]
    )


def membrane_force(edges, rest_length, moduli, rest_bend):
    nearest = edges[:, :6, :]
    stretch = jnp.sum(nearest * nearest, axis=0) / (rest_length * rest_length)
    tension = (stretch - 1.0) / (stretch + 1.0)
    surface = moduli[0] * jnp.sum((tension / rest_length)[None] * nearest, axis=1)
    bending = jnp.sum(cycle_weights()[None, :, None] * edges, axis=1) - rest_bend
    return surface + moduli[1] * bending


def evaluate(current, load):
    targets = lax.all_gather(current, "src", axis=1, tiled=True)
    partial_sum = stokes_sum(
        targets,
        lax.all_gather(current, "tgt", axis=1, tiled=True),
        lax.all_gather(load, "tgt", axis=1, tiled=True),
    )
    return lax.psum_scatter(partial_sum, "src", scatter_dimension=1, tiled=True)


def body(positions, forces, neighbours, patch_owner, rest_length, moduli, rest_bend):
    devices = lax.axis_size("tgt") * lax.axis_size("src")
    local_nodes = positions.shape[1]
    capacity = rest_length.shape[1] // devices
    owners = patch_owner[:, 0]
    onehot = (owners[:, None] == jnp.arange(devices, dtype=jnp.int32)[None, :]).astype(jnp.int32)
    before = jnp.cumsum(onehot, axis=0) - onehot
    place = owners * capacity + jnp.sum(before * onehot, axis=1)
    scale = 1.0 / math.sqrt(local_nodes * devices)
    current = positions
    load = forces
    for update in range(STEPS):
        velocity = evaluate(current, load) * scale
        current = current + time_step * velocity
        edges = current[:, neighbours] - current[:, None, :]
        outgoing = (
            jnp.zeros((36, devices * capacity), jnp.float32)
            .at[:, place]
            .set(edges.reshape(36, local_nodes))
        )
        arrived = lax.all_to_all(
            outgoing.reshape(36, devices, capacity),
            ("tgt", "src"),
            split_axis=1,
            concat_axis=1,
            tiled=True,
        )
        owned = membrane_force(
            arrived.reshape(3, 12, devices * capacity), rest_length, moduli, rest_bend
        )
        returned = lax.all_to_all(
            owned.reshape(3, devices, capacity),
            ("tgt", "src"),
            split_axis=1,
            concat_axis=1,
            tiled=True,
        )
        load = returned.reshape(3, devices * capacity)[:, place]
    velocity = evaluate(current, load) * scale
    return (current, velocity)


def solution(mesh):
    placed = (
        P(None, ("tgt", "src")),
        P(None, ("tgt", "src")),
        P(None, ("tgt", "src")),
        P(("tgt", "src"), None),
        P(None, ("tgt", "src")),
        P(None, ("tgt", "src")),
        P(None, ("tgt", "src")),
    )
    return jax.shard_map(
        body,
        mesh=mesh,
        in_specs=placed,
        out_specs=(P(None, ("tgt", "src")), P(None, ("tgt", "src"))),
        check_vma=False,
    )
```

profile of v0, /device:TPU:1, one launch (start us, length us, event | category | flops | bytes accessed | tf_op | source)
XLA Modules:
  0.0 1170.0 jit_solution(5419765780047768369)
XLA Ops:
  7.2 22.7 %all_gather.36 = f32[3,4096]{1,0:T(4,128)S(1)} all-gather(f32[3,256]{1,0:T(4,128)} %param.15), channel_id=1, replica_groups=mesh['tgt'=8,'src'=16] {'src'}, dimensions={1}, use_global_device_ids=true | all-gather | bytes 52224 | tf_op jit(solution)/shard_map/all_gather | solution.py:63
  29.9 28.1 %all_gather.37 = f32[3,2048]{1,0:T(4,128)S(1)} all-gather(f32[3,256]{1,0:T(4,128)} %param.15), channel_id=1, replica_groups=mesh['tgt'=8,'src'=16] {'tgt'}, dimensions={1}, use_global_device_ids=true | all-gather | bytes 27648 | tf_op jit(solution)/shard_map/all_gather | solution.py:66
  58.0 27.8 %all_gather.38 = f32[3,2048]{1,0:T(4,128)S(1)} all-gather(f32[3,256]{1,0:T(4,128)} %param.16), channel_id=1, replica_groups=mesh['tgt'=8,'src'=16] {'tgt'}, dimensions={1}, use_global_device_ids=true | all-gather | bytes 27648 | tf_op jit(solution)/shard_map/all_gather | solution.py:67
  85.9 95.0 %while.36 = (s32[]{:T(128)}, f32[8,3,512]{2,1,0:T(4,128)S(1)}, f32[8,3,512]{2,1,0:T(4,128)S(1)}, f32[1,3,2048]{2,1,0:T(4,128)S(1)}, f32[1,3,2048]{2,1,0:T(4,128)S(1)}, /*index=5*/s32[]{:T(128)}) while((s32[]{:T(128)}, f32[8,3,512]{2,1,0:T(4,128)S(1)}, f32[8,3,512]{2,1,0:T(4,128)S(1)}, f32[1,3,2048]{2,1,0:T(4,128)S(1)}, ...), condition=%wide.region_4.5_spmd, body=%wide.region_0.4_spmd.sunk | while | flops 35650048 | bytes 33699916 | solution.py:43
  85.9 7.4 fusion.43
  97.8 7.4 fusion.43
  109.7 7.4 fusion.43
  121.6 7.4 fusion.43
  133.4 7.4 fusion.43
  145.3 7.4 fusion.43
  157.2 7.4 fusion.43
  169.1 7.4 fusion.43
  183.8 69.3 %reduce-scatter.7.cloned.1.call-done = f32[3,256]{0,1:T(8,128)} async-done(((f32[3,4096]{0,1:T(8,128)}), f32[3,256]{0,1:T(8,128)}) %reduce-scatter.7.cloned.1.call-update) | async-done | bytes 3088 | tf_op jit(solution)/shard_map/reduce_scatter | solution.py:69
  254.1 8.1 gather_fusion
  265.7 10.9 all-to-all-start
  276.7 10.7 all-to-all-done
  290.6 2.7 reshape.279
  295.4 3.8 all-to-all-start.1
  299.3 27.6 %all_gather.39 = f32[3,4096]{0,1:T(8,128)S(1)} all-gather(f32[3,256]{0,1:T(8,128)S(1)} %multiply_add_fusion.2), channel_id=1, replica_groups=mesh['tgt'=8,'src'=16] {'src'}, dimensions={1}, use_global_device_ids=true | all-gather | bytes 52224 | tf_op jit(solution)/shard_map/all_gather | solution.py:63
  327.5 31.0 %all_gather.40 = f32[3,2048]{0,1:T(8,128)S(1)} all-gather(f32[3,256]{0,1:T(8,128)S(1)} %multiply_add_fusion.2), channel_id=1, replica_groups=mesh['tgt'=8,'src'=16] {'tgt'}, dimensions={1}, use_global_device_ids=true | all-gather | bytes 27648 | tf_op jit(solution)/shard_map/all_gather | solution.py:66
  360.1 31.3 %all-gather = f32[3,2048]{0,1:T(8,128)S(1)} all-gather(f32[3,256]{0,1:T(8,128)S(1)} %bitcast.188), channel_id=2, replica_groups=mesh['tgt'=8,'src'=16] {'tgt'}, dimensions={1}, use_global_device_ids=true | all-gather | bytes 27648 | tf_op jit(solution)/shard_map/all_gather | solution.py:67
  391.8 95.0 %while.37 = (s32[]{:T(128)}, f32[8,3,512]{2,1,0:T(4,128)S(1)}, f32[8,3,512]{2,1,0:T(4,128)S(1)}, f32[1,3,2048]{2,1,0:T(4,128)S(1)}, f32[1,3,2048]{2,1,0:T(4,128)S(1)}, /*index=5*/s32[]{:T(128)}) while((s32[]{:T(128)}, f32[8,3,512]{2,1,0:T(4,128)S(1)}, f32[8,3,512]{2,1,0:T(4,128)S(1)}, f32[1,3,2048]{2,1,0:T(4,128)S(1)}, ...), condition=%wide.region_17.18_spmd, body=%wide.region_13.17_spmd.sunk | while | flops 35650048 | bytes 33699916 | solution.py:43
  391.8 7.4 fusion.45
  403.7 7.4 fusion.45
  415.6 7.4 fusion.45
  427.5 7.4 fusion.45
  439.3 7.4 fusion.45
  451.2 7.4 fusion.45
  463.1 7.4 fusion.45
  475.0 7.4 fusion.45
  488.9 67.7 %reduce-scatter.9.cloned.1.call-done = f32[3,256]{0,1:T(8,128)} async-done(((f32[3,4096]{0,1:T(8,128)}), f32[3,256]{0,1:T(8,128)}) %reduce-scatter.9.cloned.1.call-update) | async-done | bytes 3088 | tf_op jit(solution)/shard_map/reduce_scatter | solution.py:69
  557.5 8.1 gather_fusion.2
  569.2 10.6 all-to-all-start.2
  579.8 10.8 all-to-all-done.2
  598.0 4.2 all-to-all-start.3
  602.3 27.6 %all_gather.42 = f32[3,4096]{0,1:T(8,128)S(1)} all-gather(f32[3,256]{0,1:T(8,128)S(1)} %multiply_add_fusion.1), channel_id=1, replica_groups=mesh['tgt'=8,'src'=16] {'src'}, dimensions={1}, use_global_device_ids=true | all-gather | bytes 52224 | tf_op jit(solution)/shard_map/all_gather | solution.py:63
  630.5 31.0 %all_gather.43 = f32[3,2048]{0,1:T(8,128)S(1)} all-gather(f32[3,256]{0,1:T(8,128)S(1)} %multiply_add_fusion.1), channel_id=1, replica_groups=mesh['tgt'=8,'src'=16] {'tgt'}, dimensions={1}, use_global_device_ids=true | all-gather | bytes 27648 | tf_op jit(solution)/shard_map/all_gather | solution.py:66
  663.1 31.3 %all-gather.1 = f32[3,2048]{0,1:T(8,128)S(1)} all-gather(f32[3,256]{0,1:T(8,128)S(1)} %bitcast.189), channel_id=3, replica_groups=mesh['tgt'=8,'src'=16] {'tgt'}, dimensions={1}, use_global_device_ids=true | all-gather | bytes 27648 | tf_op jit(solution)/shard_map/all_gather | solution.py:67
  694.8 95.0 %while.38 = (s32[]{:T(128)}, f32[8,3,512]{2,1,0:T(4,128)S(1)}, f32[8,3,512]{2,1,0:T(4,128)S(1)}, f32[1,3,2048]{2,1,0:T(4,128)S(1)}, f32[1,3,2048]{2,1,0:T(4,128)S(1)}, /*index=5*/s32[]{:T(128)}) while((s32[]{:T(128)}, f32[8,3,512]{2,1,0:T(4,128)S(1)}, f32[8,3,512]{2,1,0:T(4,128)S(1)}, f32[1,3,2048]{2,1,0:T(4,128)S(1)}, ...), condition=%wide.region_27.28_spmd, body=%wide.region_23.27_spmd.sunk | while | flops 35650048 | bytes 33699916 | solution.py:43
  694.8 7.4 fusion.47
  706.7 7.4 fusion.47
  718.6 7.4 fusion.47
  730.4 7.4 fusion.47
  742.3 7.4 fusion.47
  754.2 7.4 fusion.47
  766.1 7.4 fusion.47
  778.0 7.4 fusion.47
  791.9 67.7 %reduce-scatter.11.cloned.1.call-done = f32[3,256]{0,1:T(8,128)} async-done(((f32[3,4096]{0,1:T(8,128)}), f32[3,256]{0,1:T(8,128)}) %reduce-scatter.11.cloned.1.call-update) | async-done | bytes 3088 | tf_op jit(solution)/shard_map/reduce_scatter | solution.py:69
  860.5 8.1 gather_fusion.4
  871.5 21.5 %all_to_all.30 = f32[128,1,360]{2,1,0:T(1,128)S(1)} all-to-all(f32[128,1,360]{2,1,0:T(1,128)S(1)} %reshape.294), channel_id=1, replica_groups=mesh['tgt'=8,'src'=16] {'tgt','src'}, dimensions={0} | all-to-all | bytes 368640 | tf_op jit(solution)/shard_map/all_to_all | solution.py:92
  900.5 3.8 all-to-all-start.5
  904.4 27.6 %all_gather.45 = f32[3,4096]{0,1:T(8,128)S(1)} all-gather(f32[3,256]{0,1:T(8,128)S(1)} %multiply_add_fusion), channel_id=1, replica_groups=mesh['tgt'=8,'src'=16] {'src'}, dimensions={1}, use_global_device_ids=true | all-gather | bytes 52224 | tf_op jit(solution)/shard_map/all_gather | solution.py:63
  932.6 31.0 %all_gather.46 = f32[3,2048]{0,1:T(8,128)S(1)} all-gather(f32[3,256]{0,1:T(8,128)S(1)} %multiply_add_fusion), channel_id=1, replica_groups=mesh['tgt'=8,'src'=16] {'tgt'}, dimensions={1}, use_global_device_ids=true | all-gather | bytes 27648 | tf_op jit(solution)/shard_map/all_gather | solution.py:66
  965.2 31.3 %all-gather.2 = f32[3,2048]{0,1:T(8,128)S(1)} all-gather(f32[3,256]{0,1:T(8,128)S(1)} %bitcast.187), channel_id=4, replica_groups=mesh['tgt'=8,'src'=16] {'tgt'}, dimensions={1}, use_global_device_ids=true | all-gather | bytes 27648 | tf_op jit(solution)/shard_map/all_gather | solution.py:67
  996.9 95.0 %while.39 = (s32[]{:T(128)}, f32[8,3,512]{2,1,0:T(4,128)S(1)}, f32[8,3,512]{2,1,0:T(4,128)S(1)}, f32[1,3,2048]{2,1,0:T(4,128)S(1)}, f32[1,3,2048]{2,1,0:T(4,128)S(1)}, /*index=5*/s32[]{:T(128)}) while((s32[]{:T(128)}, f32[8,3,512]{2,1,0:T(4,128)S(1)}, f32[8,3,512]{2,1,0:T(4,128)S(1)}, f32[1,3,2048]{2,1,0:T(4,128)S(1)}, ...), condition=%wide.region_37.38_spmd, body=%wide.region_33.37_spmd.sunk | while | flops 35650048 | bytes 33699916 | solution.py:43
  996.9 7.4 fusion.49
  1008.8 7.4 fusion.49
  1020.7 7.4 fusion.49
  1032.5 7.4 fusion.49
  1044.4 7.4 fusion.49
  1056.3 7.4 fusion.49
  1068.2 7.4 fusion.49
  1080.0 7.4 fusion.49
  1093.9 67.7 %reduce-scatter.13.cloned.1.call-done = f32[256,3]{1,0:T(8,128)} async-done(((f32[4096,3]{1,0:T(8,128)}), f32[256,3]{1,0:T(8,128)}) %reduce-scatter.13.cloned.1.call-update) | async-done | bytes 3088
  (262 shorter events, 193.6 us)
Async XLA Ops:
  7.2 246.0 %reduce-scatter.7.cloned.1.call-start = ((), (), s32[]{:S(2)}) async-start(), calls=%async_computation.10 | async-start | bytes 2228224 | tf_op jit(solution)/shard_map/reduce_scatter | solution.py:69
  180.9 2.1 copy-start.4
  180.9 2.1 copy-start.6
  181.0 2.7 copy-start.2
  183.0 93.6 %copy-start.5 = (f32[2,1280]{1,0:T(2,128)S(1)}, f32[2,1280]{1,0:T(2,128)}, u32[]{:S(2)}) copy-start(f32[2,1280]{1,0:T(2,128)} %param.20) | copy-start | bytes 30724
  265.7 21.6 %all-to-all-start = ((f32[128,1,360]{2,1,0:T(1,128)}), f32[128,1,360]{2,1,0:T(1,128)S(1)}, u32[]{:S(2)}, u32[]{:S(2)}) async-start(f32[128,1,360]{2,1,0:T(1,128)} %reshape.290), calls=%async_computation.1 | async-start | bytes 393216 | tf_op jit(solution)/shard_map/all_to_all | solution.py:92
  276.6 17.6 %copy-start = (f32[6,1280]{1,0:T(8,128)S(1)}, f32[6,1280]{1,0:T(8,128)}, u32[]{:S(2)}) copy-start(f32[6,1280]{1,0:T(8,128)} %param.19) | copy-start | bytes 92164
  289.1 5.2 copy-start.7
  289.1 5.3 copy-start.1
  295.4 63.5 %all-to-all-start.1 = ((f32[3,128,10]{2,0,1:T(4,128)}), f32[3,128,10]{2,0,1:T(4,128)S(1)}, u32[]{:S(2)}, u32[]{:S(2)}) async-start(f32[3,128,10]{2,0,1:T(4,128)} %copy.113), calls=%async_computation.2 | async-start | bytes 524288 | tf_op jit(solution)/shard_map/all_to_all | solution.py:102
  299.3 257.3 %reduce-scatter.9.cloned.1.call-start = ((), (), s32[]{:S(2)}) async-start(), calls=%async_computation.11 | async-start | bytes 2228224 | tf_op jit(solution)/shard_map/reduce_scatter | solution.py:69
  569.2 21.4 %all-to-all-start.2 = ((f32[128,1,360]{2,1,0:T(1,128)}), f32[128,1,360]{2,1,0:T(1,128)S(1)}, u32[]{:S(2)}, u32[]{:S(2)}) async-start(f32[128,1,360]{2,1,0:T(1,128)} %reshape.292), calls=%async_computation.4 | async-start | bytes 393216 | tf_op jit(solution)/shard_map/all_to_all | solution.py:92
  598.0 63.9 %all-to-all-start.3 = ((f32[3,128,10]{2,0,1:T(4,128)}), f32[3,128,10]{2,0,1:T(4,128)S(1)}, u32[]{:S(2)}, u32[]{:S(2)}) async-start(f32[3,128,10]{2,0,1:T(4,128)} %copy.124), calls=%async_computation.5 | async-start | bytes 524288 | tf_op jit(solution)/shard_map/all_to_all | solution.py:102
  602.3 257.3 %reduce-scatter.11.cloned.1.call-start = ((), (), s32[]{:S(2)}) async-start(), calls=%async_computation.12 | async-start | bytes 2228224 | tf_op jit(solution)/shard_map/reduce_scatter | solution.py:69
  868.7 29.6 %copy-start.3 = (f32[3,256]{1,0:T(4,128)}, f32[3,256]{1,0:T(4,128)S(1)}, u32[]{:S(2)}) copy-start(f32[3,256]{1,0:T(4,128)S(1)} %copy.141) | copy-start | bytes 9220
  900.5 63.5 %all-to-all-start.5 = ((f32[3,128,10]{2,0,1:T(4,128)}), f32[3,128,10]{2,0,1:T(4,128)S(1)}, u32[]{:S(2)}, u32[]{:S(2)}) async-start(f32[3,128,10]{2,0,1:T(4,128)} %copy.135), calls=%async_computation.8 | async-start | bytes 524288 | tf_op jit(solution)/shard_map/all_to_all | solution.py:102
  904.3 257.3 %reduce-scatter.13.cloned.1.call-start = ((), (), s32[]{:S(2)}) async-start(), calls=%async_computation.13 | async-start | bytes 2228224
Sparse Core Ops, SparseCore 0:
  183.1 69.9 reduce-scatter.6
  489.0 67.5 reduce-scatter.8
  792.0 67.5 reduce-scatter.10
  1094.1 67.5 reduce-scatter.12
where the time goes:
time: 1180 us; the launch traced here: 1170 us
  other arithmetic  386 us (33%)
  blocking collectives  370 us (31%)
  waiting for transfers between devices  294 us (25%)
  local copies, waits for them, and re-layouts  70.1 us (6%)
  starting transfers between devices  33.4 us (3%)
  between operations  14.6 us (1%)
    reduce_sum x32, other arithmetic, stokes_block(): radius_sq = jnp.sum(delta * delta, axis=0)  236 us
    reduce_scatter x3, waiting for transfers between devices, evaluate(): return lax.psum_scatter(partial_sum, 'src', scatter_dimension=1, tiled=True)  205 us
    all_gather x4, blocking collectives, evaluate(): lax.all_gather(load, 'tgt', axis=1, tiled=True)  122 us
    all_gather x4, blocking collectives, evaluate(): lax.all_gather(current, 'tgt', axis=1, tiled=True)  121 us
    all_gather x4, blocking collectives, evaluate(): targets = lax.all_gather(current, 'src', axis=1, tiled=True)  106 us
    reduce_sum x32, other arithmetic, stokes_block(): jnp.sum(direct[None] * source_force[:, None, :] + tensor[None] * delta, a...  77.2 us
    unnamed x5, waiting for transfers between devices  67.8 us
    mul x32, other arithmetic, stokes_block(): direct = (radius_sq + 2.0 * blob_square) * inverse  65.1 us
  transfers between devices with their start and end apart: 9, of which 6 were waited for; matrix products, arithmetic and copies ran while one was open for 0% of the time, Pallas kernels for 0%

commit v1 on v0

v1 whole, which is shorter than its diff:
```python
import functools
import math

import jax
import jax.numpy as jnp
from jax import lax
from jax.experimental import pallas as pl
from jax.experimental.pallas import tpu as pltpu
from jax.sharding import PartitionSpec as P

F32, BF16 = jnp.float32, jnp.bfloat16
MESH = pl.DeviceIdType.MESH
STEPS = 3
EPS = 0.0025
TIME_STEP = 0.5
ROWS = 32
GROUP = 8
FIELDS = 12


def split3(v):
    high = v.astype(BF16).astype(F32)
    rest = v - high
    middle = rest.astype(BF16).astype(F32)
    return [high.astype(BF16), middle.astype(BF16), (rest - middle).astype(BF16)]


def dot(a, b, dims):
    return lax.dot_general(a, b, (dims, ((), ())), preferred_element_type=F32)


def kernel(n_src, devices, nodes, capacity, scale, pos_ref, frc_ref, nbr_ref, own_ref, par_ref, x_out, v_out,
           buf, blk, par_buf, par_own, prm, xb, acc, send_sem, recv_sem, par_send, par_recv):
    me = lax.axis_index("tgt") * n_src + lax.axis_index("src")
    groups = devices // GROUP

    def coords(k):
        t = lax.rem(me + k, devices)
        return (lax.div(t, n_src), lax.rem(t, n_src))

    barrier = pltpu.get_barrier_semaphore()

    @pl.loop(1, devices)
    def _(k):
        pl.semaphore_signal(barrier, inc=1, device_id=coords(k), device_id_type=MESH)

    zero_row = jnp.zeros((2, nodes), F32)
    blk[0] = jnp.concatenate([pos_ref[...], frc_ref[...], zero_row], axis=0)
    pl.semaphore_wait(barrier, devices - 1)

    def send_block(e):
        @pl.loop(1, devices)
        def _(k):
            pltpu.make_async_remote_copy(
                src_ref=blk.at[e], dst_ref=buf.at[e, k],
                send_sem=send_sem.at[e], recv_sem=recv_sem.at[e, lax.div(k, GROUP)],
                device_id=coords(k), device_id_type=MESH,
            ).start()

    def velocity(e):
        own = blk[e]
        buf[e, 0] = own
        parts = jnp.concatenate([p.astype(F32) for p in split3(own)], axis=0).astype(BF16)
        row = lax.broadcasted_iota(jnp.int32, (24, 128), 0)
        for c in range(3):
            pick = ((row % 8) == c).astype(F32).astype(BF16)
            xb[c] = dot(parts, pick, ((0,), (0,)))
        acc[...] = jnp.zeros_like(acc)

        @pl.loop(0, groups)
        def _(g):
            @pl.when(g == 0)
            def _():
                w = buf.at[e, pl.ds(1, GROUP - 1)]
                pltpu.make_async_remote_copy(w, w, send_sem.at[e], recv_sem.at[e, 0], device_id=coords(1), device_id_type=MESH).wait_recv()

            @pl.when(g > 0)
            def _():
                w = buf.at[e, pl.ds(g * GROUP, GROUP)]
                pltpu.make_async_remote_copy(w, w, send_sem.at[e], recv_sem.at[e, g], device_id=coords(1), device_id_type=MESH).wait_recv()

            @pl.loop(0, nodes // ROWS)
            def _(i):
                rows = pl.ds(pl.multiple_of(i * ROWS, ROWS), ROWS)
                x = [xb[c, rows, :] for c in range(3)]

                def step(j, total):
                    total = list(total)
                    for h in range(nodes // 128):
                        s = [buf[e, g * GROUP + j, c:c + 1, h * 128:(h + 1) * 128] for c in range(6)]
                        d = [x[c] - s[c] for c in range(3)]
                        q = d[0] * d[0] + (d[1] * d[1] + (d[2] * d[2] + EPS))
                        w = lax.rsqrt(q)
                        w3 = w * w * w
                        direct = w + EPS * w3
                        along = (d[0] * s[3] + d[1] * s[4] + d[2] * s[5]) * w3
                        for c in range(3):
                            total[c] = total[c] + (direct * s[3 + c] + along * d[c])
                    return tuple(total)

                total = lax.fori_loop(0, GROUP, step, tuple(acc[c, rows, :] for c in range(3)), unroll=2)
                for c in range(3):
                    acc[c, rows, :] = total[c]

        ones = jnp.ones((8, 128), BF16)
        out = []
        for c in range(3):
            h, m, l = split3(acc[c])
            out.append((dot(ones, h, ((1,), (1,))) + dot(ones, m, ((1,), (1,))) + dot(ones, l, ((1,), (1,))))[0:1])
        return jnp.concatenate(out, axis=0) * scale

    def take_params():
        w = par_buf.at[pl.ds(0, devices - 1)]
        pltpu.make_async_remote_copy(w, w, par_send, par_recv, device_id=coords(1), device_id_type=MESH).wait_recv()
        par_buf[me] = par_own[...]
        table = par_buf[...].reshape(devices, 128)
        owner = own_ref[...]
        hot = (lax.broadcasted_iota(jnp.int32, (devices, nodes), 0) == owner).astype(F32)
        hot16 = hot.astype(BF16)
        earlier = (lax.broadcasted_iota(jnp.int32, (nodes, nodes), 0) < lax.broadcasted_iota(jnp.int32, (nodes, nodes), 1))
        before = dot(hot16, earlier.astype(F32).astype(BF16), ((1,), (0,)))
        rank = jnp.sum(before * hot, axis=0, keepdims=True)
        rows = sum(dot(p, hot16, ((0,), (0,))) for p in split3(table))
        place = lax.broadcasted_iota(jnp.int32, (128, nodes), 0)
        base = rank.astype(jnp.int32) * FIELDS
        rows = jnp.where((place >= base) & (place < base + FIELDS), rows, 0.0)
        fold = ((lax.broadcasted_iota(jnp.int32, (16, 128), 1) % FIELDS) == lax.broadcasted_iota(jnp.int32, (16, 128), 0))
        fold = fold.astype(F32).astype(BF16)
        prm[...] = sum(dot(fold, p, ((1,), (0,))) for p in split3(rows))

    def membrane(x):
        length, modulus, bend = prm[0:6], prm[6:8], prm[8:11]
        index = nbr_ref[...]
        index = jnp.concatenate([index, index[:4]], axis=0)
        edges = []
        for c in range(3):
            halves = []
            for h in range(nodes // 128):
                where = index[:, h * 128:(h + 1) * 128]
                low = lax.rem(where, 128)
                got = None
                for s in range(nodes // 128):
                    pool = jnp.broadcast_to(x[c:c + 1, s * 128:(s + 1) * 128], (16, 128))
                    one = jnp.concatenate([jnp.take_along_axis(pool[k:k + 8], low[k:k + 8], axis=1) for k in (0, 8)], axis=0)
                    got = one if got is None else jnp.where(where >= s * 128, one, got)
                halves.append(got)
            edges.append(jnp.concatenate(halves, axis=1)[:12] - x[c:c + 1])
        square = edges[0][:6] ** 2 + edges[1][:6] ** 2 + edges[2][:6] ** 2
        stretch = square / (length * length)
        tension = (stretch - 1.0) / (stretch + 1.0) / length
        out = []
        for c in range(3):
            surface = modulus[0:1] * jnp.sum(tension * edges[c][:6], axis=0, keepdims=True)
            near = jnp.sum(edges[c][:6], axis=0, keepdims=True) * (2.0 / 9.0)
            far = jnp.sum(edges[c][6:], axis=0, keepdims=True) * (1.0 / 18.0)
            out.append(surface + modulus[1:2] * (near - far - bend[c:c + 1]))
        return jnp.concatenate(out, axis=0)

    send_block(0)
    par_own[...] = par_ref[me]

    @pl.loop(1, devices)
    def _(k):
        t = lax.rem(me + k, devices)
        pltpu.make_async_remote_copy(
            src_ref=par_ref.at[t], dst_ref=par_buf.at[me], send_sem=par_send, recv_sem=par_recv,
            device_id=coords(k), device_id_type=MESH,
        ).start()

    @pl.loop(0, STEPS)
    def _(e):
        u = velocity(e)
        x = blk[e][0:3] + TIME_STEP * u

        @pl.when(e == 0)
        def _():
            take_params()

        blk[e + 1] = jnp.concatenate([x, membrane(x), zero_row], axis=0)
        send_block(e + 1)

    x_out[...] = blk[STEPS][0:3]
    v_out[...] = velocity(STEPS)
    for e in range(STEPS + 1):
        w = buf.at[e, pl.ds(1, devices - 1)]
        pltpu.make_async_remote_copy(w, w, send_sem.at[e], recv_sem.at[e, 0], device_id=coords(1), device_id_type=MESH).wait_send()
    w = par_buf.at[pl.ds(0, devices - 1)]
    pltpu.make_async_remote_copy(w, w, par_send, par_recv, device_id=coords(1), device_id_type=MESH).wait_send()


def solution(mesh):
    n_tgt, n_src = mesh.shape["tgt"], mesh.shape["src"]
    devices = n_tgt * n_src

    def body(positions, forces, neighbours, patch_owner, rest_length, moduli, rest_bend):
        nodes = positions.shape[1]
        capacity = rest_length.shape[1] // devices
        fields = jnp.concatenate([rest_length, moduli, rest_bend, jnp.zeros_like(moduli[:1])], axis=0)
        table = fields.reshape(FIELDS, devices, capacity).transpose(1, 2, 0).reshape(devices, 1, capacity * FIELDS)
        table = jnp.pad(table, ((0, 0), (0, 0), (0, 128 - capacity * FIELDS)))
        vmem = pl.BlockSpec(memory_space=pltpu.VMEM)
        return pl.pallas_call(
            functools.partial(kernel, n_src, devices, nodes, capacity, 1.0 / math.sqrt(nodes * devices)),
            name="stokes",
            out_shape=(jax.ShapeDtypeStruct((3, nodes), F32), jax.ShapeDtypeStruct((3, nodes), F32)),
            in_specs=[vmem] * 5,
            out_specs=(vmem, vmem),
            scratch_shapes=[
                pltpu.VMEM((STEPS + 1, devices, 8, nodes), F32),
                pltpu.VMEM((STEPS + 1, 8, nodes), F32),
                pltpu.VMEM((devices, 1, 128), F32),
                pltpu.VMEM((1, 128), F32),
                pltpu.VMEM((16, nodes), F32),
                pltpu.VMEM((3, nodes, 128), F32),
                pltpu.VMEM((3, nodes, 128), F32),
                pltpu.SemaphoreType.DMA((STEPS + 1,)),
                pltpu.SemaphoreType.DMA((STEPS + 1, devices // GROUP)),
                pltpu.SemaphoreType.DMA,
                pltpu.SemaphoreType.DMA,
            ],
            compiler_params=pltpu.CompilerParams(collective_id=0, has_side_effects=True, vmem_limit_bytes=48 * 1024 * 1024),
        )(positions, forces, neighbours, patch_owner.reshape(1, nodes), table)

    cut = P(None, ("tgt", "src"))
    return jax.shard_map(
        body,
        mesh=mesh,
        in_specs=(cut, cut, cut, P(("tgt", "src"), None), cut, cut, cut),
        out_specs=(cut, cut),
        check_vma=False,
    )
```

time: 1180 us -> 214 us (0.18)
  other arithmetic: 386 us -> 0.89 us
  blocking collectives: 370 us -> 0 us
  waiting for transfers between devices: 294 us -> 0 us
  Pallas kernels: 0 us -> 205 us
  local copies, waits for them, and re-layouts: 70.1 us -> 3.17 us
  starting transfers between devices: 33.4 us -> 0 us
  between operations: 14.6 us -> 0.7 us
    all_gather x12 -> x0, blocking collectives: 349 us -> none  [the longest x4 122 us: evaluate(): lax.all_gather(load, 'tgt', axis=1, tiled=True)]
    reduce_sum x74 -> x0, other arithmetic: 314 us -> none  [the longest x32 236 us: stokes_block(): radius_sq = jnp.sum(delta * delta, axis=0)]
    pallas_call x0 -> x1, Pallas kernels: none -> 205 us  [body(): pl.pallas_call(functools.partial(kernel, n_src, devices, nodes, capacity,...]
    reduce_scatter x3 -> x0, waiting for transfers between devices: 205 us -> none  [evaluate(): return lax.psum_scatter(partial_sum, 'src', scatter_dimension=1, tiled=True)]
    unnamed x5 -> x0, waiting for transfers between devices: 67.8 us -> none
    mul x33 -> x0, other arithmetic: 65.7 us -> none  [the longest x32 65.1 us: stokes_block(): direct = (radius_sq + 2.0 * blob_square) * inverse]
    all_to_all x5 -> x0, starting transfers between devices: 33.3 us -> none  [the longest x2 21.4 us: body(): lax.all_to_all(outgoing.reshape(36, devices, capacity), ('tgt', 'src'), s...]
    gather x9 -> x0, local copies, waits for them, and re-layouts: 28.5 us -> none  [the longest x6 26.3 us: body(): edges = current[:, neighbours] - current[:, None, :]]
  transfers between devices with their start and end apart: 9 -> 0, of which waited for: 6 -> 0; matrix products, arithmetic and copies ran while one was open for 0% -> 0% of each run, Pallas kernels for 0% -> 0%
where the time goes in v1:
time: 214 us; the launch traced here: 210 us
  Pallas kernels  205 us (96%)
  local copies, waits for them, and re-layouts  3.17 us (1%)
    pallas_call x1, Pallas kernels, body(): pl.pallas_call(functools.partial(kernel, n_src, devices, nodes, capacity,...  205 us

profile of v1, /device:TPU:1, one launch (start us, length us, event | category | flops | bytes accessed | tf_op | source)
XLA Modules:
  0.0 209.9 jit_solution(5724395510295487179)
XLA Ops:
  0.6 0.1 pad.8.clone
  0.7 0.9 maximum_maximum_fusion
  1.6 0.8 reshape.14
  2.4 0.3 copy.10
  2.7 0.1 copy.11
  2.8 0.0 copy-start
  2.8 0.0 copy-start.1
  2.9 0.0 copy-start.2
  2.9 0.0 copy-start.3
  2.9 0.6 copy-done
  3.6 0.0 copy-done.1
  3.6 0.0 copy-done.2
  3.6 0.0 copy-done.3
  3.6 205.2 %stokes.1 = (f32[3,256]{1,0:T(4,128)S(1)}, f32[3,256]{1,0:T(4,128)S(1)}) custom-call(f32[3,256]{1,0:T(4,128)S(1)} %copy-done.1, f32[3,256]{1,0:T(4,128)S(1)} %copy-done.2, s32[12,256]{1,0:T(8,128)S(1)} %copy-done, s32[1,256]{1,0:T(1,128)S(1)} %bitcast.5, f32[128,1,128]{2,1,0:T(1,128)S(1)} %pad.4.par_ref), custom_call_target="tpu_custom_call" | custom-call | tf_op jit(solution)/shard_map/stokes/pallas_call | solution.py:202
  208.7 0.6 copy.14
  209.3 0.6 copy.15
  (2 shorter events, 0.1 us)
Async XLA Ops:
  2.8 0.7 copy-start
  2.8 0.7 copy-start.1
  2.9 0.7 copy-start.2
  2.9 0.7 copy-start.3

commit v2 on v1

--- a/solution.py
+++ b/solution.py
@@ -13,7 +13,7 @@
 STEPS = 3
 EPS = 0.0025
 TIME_STEP = 0.5
-ROWS = 32
+ROWS = 16
 GROUP = 8
 FIELDS = 12
 
@@ -30,9 +30,10 @@
 
 
 def kernel(n_src, devices, nodes, capacity, scale, pos_ref, frc_ref, nbr_ref, own_ref, par_ref, x_out, v_out,
-           buf, blk, par_buf, par_own, prm, xb, acc, send_sem, recv_sem, par_send, par_recv):
+           buf, blk, ret, out, par_buf, par_own, prm, xb, lhs, prod, acc, near, send_sem, recv_sem, ret_send, ret_recv, par_send, par_recv):
     me = lax.axis_index("tgt") * n_src + lax.axis_index("src")
-    groups = devices // GROUP
+    half = devices // 2
+    groups = half // GROUP
 
     def coords(k):
         t = lax.rem(me + k, devices)
@@ -44,70 +45,159 @@
     def _(k):
         pl.semaphore_signal(barrier, inc=1, device_id=coords(k), device_id_type=MESH)
 
-    zero_row = jnp.zeros((2, nodes), F32)
-    blk[0] = jnp.concatenate([pos_ref[...], frc_ref[...], zero_row], axis=0)
+    def pack(x, f):
+        return jnp.concatenate([x, f, jnp.sum(x * f, axis=0, keepdims=True), jnp.ones((1, nodes), F32)], axis=0)
+
+    blk[0] = pack(pos_ref[...], frc_ref[...])
     pl.semaphore_wait(barrier, devices - 1)
 
     def send_block(e):
-        @pl.loop(1, devices)
+        @pl.loop(0, half)
         def _(k):
             pltpu.make_async_remote_copy(
                 src_ref=blk.at[e], dst_ref=buf.at[e, k],
                 send_sem=send_sem.at[e], recv_sem=recv_sem.at[e, lax.div(k, GROUP)],
-                device_id=coords(k), device_id_type=MESH,
+                device_id=coords(k + 1), device_id_type=MESH,
             ).start()
+
+    def wait_group(e, g):
+        w = buf.at[e, pl.ds(g * GROUP, GROUP)]
+        pltpu.make_async_remote_copy(w, w, send_sem.at[e], recv_sem.at[e, g], device_id=coords(1), device_id_type=MESH).wait_recv()
+
+    def slot(s):
+        g = lax.div(s, GROUP)
+        g = jnp.where(g == 0, 0, jnp.where(g == groups - 1, 1, g + 1))
+        return g * GROUP + lax.rem(s, GROUP), g
+
+    def send_params(first, count):
+        @pl.loop(first, first + count)
+        def _(k):
+            t = lax.rem(me + k, devices)
+
+            @pl.when(k < devices)
+            def _():
+                pltpu.make_async_remote_copy(
+                    src_ref=par_ref.at[t], dst_ref=par_buf.at[me], send_sem=par_send, recv_sem=par_recv,
+                    device_id=coords(k), device_id_type=MESH,
+                ).start()
 
     def velocity(e):
         own = blk[e]
-        buf[e, 0] = own
-        parts = jnp.concatenate([p.astype(F32) for p in split3(own)], axis=0).astype(BF16)
+        own_parts = split3(own)
+        parts = jnp.concatenate([p.astype(F32) for p in own_parts], axis=0).astype(BF16)
         row = lax.broadcasted_iota(jnp.int32, (24, 128), 0)
         for c in range(3):
             pick = ((row % 8) == c).astype(F32).astype(BF16)
             xb[c] = dot(parts, pick, ((0,), (0,)))
+        none = jnp.zeros((3, nodes), F32)
+        one = jnp.ones((1, nodes), F32)
+        fields = (jnp.concatenate([none, own[0:3], -one, one * 0.0], axis=0),
+                  jnp.concatenate([-own[3:6], none, one * 0.0, own[6:7]], axis=0))
+        for i, field in enumerate(fields):
+            h, m, l = [p.astype(F32) for p in split3(field)]
+            lhs[i * nodes:(i + 1) * nodes, :] = jnp.concatenate([h, h, m, m, h, l], axis=0).T.astype(BF16)
         acc[...] = jnp.zeros_like(acc)
-
-        @pl.loop(0, groups)
-        def _(g):
-            @pl.when(g == 0)
-            def _():
-                w = buf.at[e, pl.ds(1, GROUP - 1)]
-                pltpu.make_async_remote_copy(w, w, send_sem.at[e], recv_sem.at[e, 0], device_id=coords(1), device_id_type=MESH).wait_recv()
-
-            @pl.when(g > 0)
-            def _():
-                w = buf.at[e, pl.ds(g * GROUP, GROUP)]
-                pltpu.make_async_remote_copy(w, w, send_sem.at[e], recv_sem.at[e, g], device_id=coords(1), device_id_type=MESH).wait_recv()
-
-            @pl.loop(0, nodes // ROWS)
-            def _(i):
-                rows = pl.ds(pl.multiple_of(i * ROWS, ROWS), ROWS)
-                x = [xb[c, rows, :] for c in range(3)]
-
-                def step(j, total):
-                    total = list(total)
-                    for h in range(nodes // 128):
-                        s = [buf[e, g * GROUP + j, c:c + 1, h * 128:(h + 1) * 128] for c in range(6)]
-                        d = [x[c] - s[c] for c in range(3)]
-                        q = d[0] * d[0] + (d[1] * d[1] + (d[2] * d[2] + EPS))
-                        w = lax.rsqrt(q)
-                        w3 = w * w * w
-                        direct = w + EPS * w3
-                        along = (d[0] * s[3] + d[1] * s[4] + d[2] * s[5]) * w3
+        near[...] = jnp.zeros_like(near)
+
+        def expand(g):
+            h, m, l = [p.astype(F32) for p in split3(g)]
+            return jnp.concatenate([h, m, h, m, l, h], axis=0).astype(BF16), jnp.concatenate([h, m], axis=0).astype(BF16)
+
+        def products(g, p):
+            prod[p] = dot(lhs[...], expand(g)[0], ((1,), (0,)))
+
+        def pair(g, p, both):
+            mine = expand(blk[e])[1]
+            theirs = expand(g)[1]
+            high, low = [], []
+            back = [[None] * 3 for _ in range(nodes // 128)]
+            for r in range(0, nodes, ROWS):
+                rows = slice(r, r + ROWS)
+                total = [acc[c, rows, :] for c in range(3)]
+                highs, lows = [], []
+                for h in range(nodes // 128):
+                    cols = slice(h * 128, (h + 1) * 128)
+                    d = [xb[c, rows, :] - g[c:c + 1, cols] for c in range(3)]
+                    q = d[0] * d[0] + (d[1] * d[1] + (d[2] * d[2] + EPS))
+                    w = lax.rsqrt(q)
+                    w3 = w * w * w
+                    direct = w + EPS * w3
+                    t = prod[p, rows, cols] * w3
+                    for c in range(3):
+                        total[c] = total[c] + t * d[c]
+                    if both:
+                        t = prod[p, nodes + r:nodes + r + ROWS, cols] * w3
                         for c in range(3):
-                            total[c] = total[c] + (direct * s[3 + c] + along * d[c])
-                    return tuple(total)
-
-                total = lax.fori_loop(0, GROUP, step, tuple(acc[c, rows, :] for c in range(3)), unroll=2)
+                            v = t * d[c]
+                            for k in range(0, ROWS, 8):
+                                back[h][c] = v[k:k + 8] if back[h][c] is None else back[h][c] + v[k:k + 8]
+                    top = direct.astype(BF16)
+                    highs.append(top)
+                    lows.append((direct - top.astype(F32)).astype(BF16))
                 for c in range(3):
                     acc[c, rows, :] = total[c]
+                high.append(jnp.concatenate(highs, axis=1))
+                low.append(jnp.concatenate(lows, axis=1))
+            high, low = jnp.concatenate(high, axis=0), jnp.concatenate(low, axis=0)
+            near[...] += dot(theirs, high, ((1,), (1,))) + dot(theirs, low, ((1,), (1,)))
+            if not both:
+                return None
+            rev = dot(mine, high, ((1,), (0,))) + dot(mine, low, ((1,), (0,)))
+            along = [jnp.concatenate([jnp.sum(b[c], axis=0, keepdims=True) for b in back], axis=1) for c in range(3)]
+            return jnp.concatenate(along, axis=0) + rev[3:6] + rev[11:14]
+
+        def give_back(s):
+            k, _ = slot(s)
+
+            @pl.when(k < half - 1)
+            def _():
+                pltpu.make_async_remote_copy(
+                    src_ref=out.at[e, k], dst_ref=ret.at[e, k],
+                    send_sem=ret_send.at[e], recv_sem=ret_recv.at[e],
+                    device_id=coords(devices - 1 - k), device_id_type=MESH,
+                ).start()
+
+        wait_group(e, 0)
+        products(buf[e, 0], 0)
+
+        @pl.loop(0, half // 2)
+        def _(m):
+            s = m * 2
+
+            @pl.when((lax.rem(m, GROUP // 2) == GROUP // 2 - 1) & (m < half // 2 - 1))
+            def _():
+                wait_group(e, slot(s + 2)[1])
+
+            @pl.when(m > 0)
+            def _():
+                give_back(s - 2)
+                give_back(s - 1)
+
+            if e is not STEPS:
+                @pl.when(e == 0)
+                def _():
+                    send_params(1 + m * 4, 4)
+
+            k0, k1 = slot(s)[0], slot(s + 1)[0]
+            k2 = slot(jnp.minimum(s + 2, half - 1))[0]
+            products(buf[e, k1], 1)
+            out[e, k0] = pair(buf[e, k0], 0, True)
+            products(jnp.where(m < half // 2 - 1, buf[e, k2], blk[e]), 0)
+            out[e, k1] = pair(buf[e, k1], 1, True)
+
+        give_back(half - 2)
+        give_back(half - 1)
+        pair(blk[e], 0, False)
 
         ones = jnp.ones((8, 128), BF16)
-        out = []
+        total = []
         for c in range(3):
-            h, m, l = split3(acc[c])
-            out.append((dot(ones, h, ((1,), (1,))) + dot(ones, m, ((1,), (1,))) + dot(ones, l, ((1,), (1,))))[0:1])
-        return jnp.concatenate(out, axis=0) * scale
+            total.append(sum(dot(ones, p, ((1,), (1,))) for p in split3(acc[c]))[0:1])
+        total = jnp.concatenate(total, axis=0) + near[3:6] + near[11:14]
+        w = ret.at[e, pl.ds(0, half - 1)]
+        pltpu.make_async_remote_copy(w, w, ret_send.at[e], ret_recv.at[e], device_id=coords(1), device_id_type=MESH).wait_recv()
+        total = total + jnp.sum(ret[e, 0:half - 1], axis=0)
+        return total * scale
 
     def take_params():
         w = par_buf.at[pl.ds(0, devices - 1)]
@@ -159,14 +249,6 @@
     send_block(0)
     par_own[...] = par_ref[me]
 
-    @pl.loop(1, devices)
-    def _(k):
-        t = lax.rem(me + k, devices)
-        pltpu.make_async_remote_copy(
-            src_ref=par_ref.at[t], dst_ref=par_buf.at[me], send_sem=par_send, recv_sem=par_recv,
-            device_id=coords(k), device_id_type=MESH,
-        ).start()
-
     @pl.loop(0, STEPS)
     def _(e):
         u = velocity(e)
@@ -176,14 +258,16 @@
         def _():
             take_params()
 
-        blk[e + 1] = jnp.concatenate([x, membrane(x), zero_row], axis=0)
+        blk[e + 1] = pack(x, membrane(x))
         send_block(e + 1)
 
     x_out[...] = blk[STEPS][0:3]
     v_out[...] = velocity(STEPS)
     for e in range(STEPS + 1):
-        w = buf.at[e, pl.ds(1, devices - 1)]
+        w = buf.at[e]
         pltpu.make_async_remote_copy(w, w, send_sem.at[e], recv_sem.at[e, 0], device_id=coords(1), device_id_type=MESH).wait_send()
+        w = ret.at[e, pl.ds(0, half - 1)]
+        pltpu.make_async_remote_copy(w, w, ret_send.at[e], ret_recv.at[e], device_id=coords(1), device_id_type=MESH).wait_send()
     w = par_buf.at[pl.ds(0, devices - 1)]
     pltpu.make_async_remote_copy(w, w, par_send, par_recv, device_id=coords(1), device_id_type=MESH).wait_send()
 
@@ -206,15 +290,22 @@
             in_specs=[vmem] * 5,
             out_specs=(vmem, vmem),
             scratch_shapes=[
-                pltpu.VMEM((STEPS + 1, devices, 8, nodes), F32),
+                pltpu.VMEM((STEPS + 1, devices // 2, 8, nodes), F32),
                 pltpu.VMEM((STEPS + 1, 8, nodes), F32),
+                pltpu.VMEM((STEPS + 1, devices // 2, 3, nodes), F32),
+                pltpu.VMEM((STEPS + 1, devices // 2, 3, nodes), F32),
                 pltpu.VMEM((devices, 1, 128), F32),
                 pltpu.VMEM((1, 128), F32),
                 pltpu.VMEM((16, nodes), F32),
                 pltpu.VMEM((3, nodes, 128), F32),
+                pltpu.VMEM((2 * nodes, 48), BF16),
+                pltpu.VMEM((2, 2 * nodes, nodes), F32),
                 pltpu.VMEM((3, nodes, 128), F32),
+                pltpu.VMEM((16, nodes), F32),
                 pltpu.SemaphoreType.DMA((STEPS + 1,)),
-                pltpu.SemaphoreType.DMA((STEPS + 1, devices // GROUP)),
+                pltpu.SemaphoreType.DMA((STEPS + 1, devices // 2 // GROUP)),
+                pltpu.SemaphoreType.DMA((STEPS + 1,)),
+                pltpu.SemaphoreType.DMA((STEPS + 1,)),
                 pltpu.SemaphoreType.DMA,
                 pltpu.SemaphoreType.DMA,
             ],

time: 214 us -> 159 us (0.74); the launches traced: 210 us -> 158 us
  Pallas kernels: 205 us -> 153 us
    pallas_call x1, Pallas kernels: 205 us -> 153 us  [body(): pl.pallas_call(functools.partial(kernel, n_src, devices, nodes, capacity,...]
where the time goes in v2:
time: 159 us; the launch traced here: 158 us
  Pallas kernels  153 us (96%)
  local copies, waits for them, and re-layouts  3.17 us (2%)
    pallas_call x1, Pallas kernels, body(): pl.pallas_call(functools.partial(kernel, n_src, devices, nodes, capacity,...  153 us

profile of v2, /device:TPU:1, one launch (start us, length us, event | category | flops | bytes accessed | tf_op | source)
XLA Modules:
  0.0 157.9 jit_solution(4243853188728072352)
XLA Ops:
  0.6 0.1 pad.8.clone
  0.7 0.9 maximum_maximum_fusion
  1.6 0.8 reshape.14
  2.4 0.3 copy.10
  2.7 0.1 copy.11
  2.8 0.0 copy-start
  2.8 0.0 copy-start.1
  2.9 0.0 copy-start.2
  2.9 0.0 copy-start.3
  2.9 0.6 copy-done
  3.6 0.0 copy-done.1
  3.6 0.0 copy-done.2
  3.6 0.0 copy-done.3
  3.6 153.2 %stokes.1 = (f32[3,256]{1,0:T(4,128)S(1)}, f32[3,256]{1,0:T(4,128)S(1)}) custom-call(f32[3,256]{1,0:T(4,128)S(1)} %copy-done.1, f32[3,256]{1,0:T(4,128)S(1)} %copy-done.2, s32[12,256]{1,0:T(8,128)S(1)} %copy-done, s32[1,256]{1,0:T(1,128)S(1)} %bitcast.5, f32[128,1,128]{2,1,0:T(1,128)S(1)} %pad.4.par_ref), custom_call_target="tpu_custom_call" | custom-call | tf_op jit(solution)/shard_map/stokes/pallas_call | solution.py:286
  156.8 0.6 copy.14
  157.4 0.6 copy.15
  (2 shorter events, 0.1 us)
Async XLA Ops:
  2.8 0.7 copy-start
  2.8 0.7 copy-start.1
  2.9 0.7 copy-start.2
  2.9 0.7 copy-start.3

commit v3 on v2

--- a/solution.py
+++ b/solution.py
@@ -14,7 +14,8 @@
 EPS = 0.0025
 TIME_STEP = 0.5
 ROWS = 16
-GROUP = 8
+GROUP = 4
+NEAR = 8
 FIELDS = 12
 
 
@@ -35,15 +36,24 @@
     half = devices // 2
     groups = half // GROUP
 
+    shift = n_src.bit_length() - 1
+
     def coords(k):
-        t = lax.rem(me + k, devices)
-        return (lax.div(t, n_src), lax.rem(t, n_src))
+        t = (me + k) & (devices - 1)
+        return (t >> shift, t & (n_src - 1))
 
     barrier = pltpu.get_barrier_semaphore()
 
-    @pl.loop(1, devices)
+    def greet(k):
+        pl.semaphore_signal(barrier, inc=1, device_id=coords(k), device_id_type=MESH)
+
+    @pl.loop(0, devices // 8 - 1)
     def _(k):
-        pl.semaphore_signal(barrier, inc=1, device_id=coords(k), device_id_type=MESH)
+        for i in range(1, 9):
+            greet(k * 8 + i)
+
+    for i in range(devices - 7, devices):
+        greet(i)
 
     def pack(x, f):
         return jnp.concatenate([x, f, jnp.sum(x * f, axis=0, keepdims=True), jnp.ones((1, nodes), F32)], axis=0)
@@ -51,28 +61,43 @@
     blk[0] = pack(pos_ref[...], frc_ref[...])
     pl.semaphore_wait(barrier, devices - 1)
 
+    span = (half - NEAR) // NEAR
+
+    def offset(t):
+        return NEAR + 1 + lax.rem(t, span) * NEAR + lax.div(t, span)
+
+
     def send_block(e):
-        @pl.loop(0, half)
-        def _(k):
+        def send(s, k):
             pltpu.make_async_remote_copy(
-                src_ref=blk.at[e], dst_ref=buf.at[e, k],
-                send_sem=send_sem.at[e], recv_sem=recv_sem.at[e, lax.div(k, GROUP)],
-                device_id=coords(k + 1), device_id_type=MESH,
+                src_ref=blk.at[e], dst_ref=buf.at[e, s],
+                send_sem=send_sem.at[e], recv_sem=recv_sem.at[e, s // GROUP],
+                device_id=coords(k), device_id_type=MESH,
             ).start()
+
+        for i in range(NEAR // 2):
+            send(i, i + 1)
+
+        @pl.loop(0, span)
+        def _(b):
+            for a in range(NEAR):
+                send(b * NEAR + NEAR // 2 + a, offset(b * NEAR + a))
+
+        for i in range(NEAR // 2):
+            send(half - NEAR // 2 + i, NEAR // 2 + 1 + i)
 
     def wait_group(e, g):
         w = buf.at[e, pl.ds(g * GROUP, GROUP)]
         pltpu.make_async_remote_copy(w, w, send_sem.at[e], recv_sem.at[e, g], device_id=coords(1), device_id_type=MESH).wait_recv()
 
-    def slot(s):
-        g = lax.div(s, GROUP)
-        g = jnp.where(g == 0, 0, jnp.where(g == groups - 1, 1, g + 1))
-        return g * GROUP + lax.rem(s, GROUP), g
+    def partner(s):
+        far = offset(s - NEAR // 2)
+        return jnp.where(s < NEAR // 2, s + 1, jnp.where(s >= half - NEAR // 2, s - half + NEAR + 1, far))
 
     def send_params(first, count):
         @pl.loop(first, first + count)
         def _(k):
-            t = lax.rem(me + k, devices)
+            t = (me + k) & (devices - 1)
 
             @pl.when(k < devices)
             def _():
@@ -147,14 +172,14 @@
             return jnp.concatenate(along, axis=0) + rev[3:6] + rev[11:14]
 
         def give_back(s):
-            k, _ = slot(s)
-
-            @pl.when(k < half - 1)
+            k = partner(s)
+
+            @pl.when(k < half)
             def _():
                 pltpu.make_async_remote_copy(
-                    src_ref=out.at[e, k], dst_ref=ret.at[e, k],
+                    src_ref=out.at[e, s], dst_ref=ret.at[e, k - 1],
                     send_sem=ret_send.at[e], recv_sem=ret_recv.at[e],
-                    device_id=coords(devices - 1 - k), device_id_type=MESH,
+                    device_id=coords(devices - k), device_id_type=MESH,
                 ).start()
 
         wait_group(e, 0)
@@ -166,7 +191,7 @@
 
             @pl.when((lax.rem(m, GROUP // 2) == GROUP // 2 - 1) & (m < half // 2 - 1))
             def _():
-                wait_group(e, slot(s + 2)[1])
+                wait_group(e, lax.div(s, GROUP) + 1)
 
             @pl.when(m > 0)
             def _():
@@ -178,12 +203,10 @@
                 def _():
                     send_params(1 + m * 4, 4)
 
-            k0, k1 = slot(s)[0], slot(s + 1)[0]
-            k2 = slot(jnp.minimum(s + 2, half - 1))[0]
-            products(buf[e, k1], 1)
-            out[e, k0] = pair(buf[e, k0], 0, True)
-            products(jnp.where(m < half // 2 - 1, buf[e, k2], blk[e]), 0)
-            out[e, k1] = pair(buf[e, k1], 1, True)
+            products(buf[e, s + 1], 1)
+            out[e, s] = pair(buf[e, s], 0, True)
+            products(jnp.where(m < half // 2 - 1, buf[e, jnp.minimum(s + 2, half - 1)], blk[e]), 0)
+            out[e, s + 1] = pair(buf[e, s + 1], 1, True)
 
         give_back(half - 2)
         give_back(half - 1)

time: 159 us -> 152 us (0.956)
  Pallas kernels: 153 us -> 147 us
    pallas_call x1, Pallas kernels: 153 us -> 147 us  [body(): pl.pallas_call(functools.partial(kernel, n_src, devices, nodes, capacity,...]
where the time goes in v3:
time: 152 us
  Pallas kernels  147 us (97%)
  local copies, waits for them, and re-layouts  3.17 us (2%)
    pallas_call x1, Pallas kernels, body(): pl.pallas_call(functools.partial(kernel, n_src, devices, nodes, capacity,...  147 us

profile of v3, /device:TPU:1, one launch (start us, length us, event | category | flops | bytes accessed | tf_op | source)
XLA Modules:
  0.0 151.6 jit_solution(11482982033841918386)
XLA Ops:
  0.6 0.1 pad.8.clone
  0.7 0.9 maximum_maximum_fusion
  1.6 0.8 reshape.14
  2.4 0.3 copy.10
  2.7 0.1 copy.11
  2.8 0.0 copy-start
  2.8 0.0 copy-start.1
  2.9 0.0 copy-start.2
  2.9 0.0 copy-start.3
  2.9 0.6 copy-done
  3.6 0.0 copy-done.1
  3.6 0.0 copy-done.2
  3.6 0.0 copy-done.3
  3.6 146.9 %stokes.1 = (f32[3,256]{1,0:T(4,128)S(1)}, f32[3,256]{1,0:T(4,128)S(1)}) custom-call(f32[3,256]{1,0:T(4,128)S(1)} %copy-done.1, f32[3,256]{1,0:T(4,128)S(1)} %copy-done.2, s32[12,256]{1,0:T(8,128)S(1)} %copy-done, s32[1,256]{1,0:T(1,128)S(1)} %bitcast.5, f32[128,1,128]{2,1,0:T(1,128)S(1)} %pad.4.par_ref), custom_call_target="tpu_custom_call" | custom-call | tf_op jit(solution)/shard_map/stokes/pallas_call | solution.py:309
  150.4 0.6 copy.14
  151.0 0.6 copy.15
  (2 shorter events, 0.1 us)
Async XLA Ops:
  2.8 0.7 copy-start
  2.8 0.7 copy-start.1
  2.9 0.7 copy-start.2
  2.9 0.7 copy-start.3

commit v4 on v3

--- a/solution.py
+++ b/solution.py
@@ -14,8 +14,8 @@
 EPS = 0.0025
 TIME_STEP = 0.5
 ROWS = 16
-GROUP = 4
-NEAR = 8
+NEAR = 4
+AHEAD = 16
 FIELDS = 12
 
 
@@ -34,7 +34,6 @@
            buf, blk, ret, out, par_buf, par_own, prm, xb, lhs, prod, acc, near, send_sem, recv_sem, ret_send, ret_recv, par_send, par_recv):
     me = lax.axis_index("tgt") * n_src + lax.axis_index("src")
     half = devices // 2
-    groups = half // GROUP
 
     shift = n_src.bit_length() - 1
 
@@ -61,38 +60,26 @@
     blk[0] = pack(pos_ref[...], frc_ref[...])
     pl.semaphore_wait(barrier, devices - 1)
 
-    span = (half - NEAR) // NEAR
-
-    def offset(t):
-        return NEAR + 1 + lax.rem(t, span) * NEAR + lax.div(t, span)
-
-
-    def send_block(e):
-        def send(s, k):
-            pltpu.make_async_remote_copy(
-                src_ref=blk.at[e], dst_ref=buf.at[e, s],
-                send_sem=send_sem.at[e], recv_sem=recv_sem.at[e, s // GROUP],
-                device_id=coords(k), device_id_type=MESH,
-            ).start()
-
-        for i in range(NEAR // 2):
-            send(i, i + 1)
-
-        @pl.loop(0, span)
-        def _(b):
-            for a in range(NEAR):
-                send(b * NEAR + NEAR // 2 + a, offset(b * NEAR + a))
-
-        for i in range(NEAR // 2):
-            send(half - NEAR // 2 + i, NEAR // 2 + 1 + i)
-
-    def wait_group(e, g):
-        w = buf.at[e, pl.ds(g * GROUP, GROUP)]
-        pltpu.make_async_remote_copy(w, w, send_sem.at[e], recv_sem.at[e, g], device_id=coords(1), device_id_type=MESH).wait_recv()
-
     def partner(s):
-        far = offset(s - NEAR // 2)
-        return jnp.where(s < NEAR // 2, s + 1, jnp.where(s >= half - NEAR // 2, s - half + NEAR + 1, far))
+        t = s - NEAR - 1
+        far = 2 * NEAR + 1 + (t & 7) * ((half - 2 * NEAR) // 8) + (t >> 3)
+        near_by = jnp.where(s == half, half, s - half + 2 * NEAR + 1)
+        return jnp.where(s <= NEAR, s, jnp.where(s >= half - NEAR, near_by, far))
+
+    def send_block(e, s):
+        pltpu.make_async_remote_copy(
+            src_ref=blk.at[e, pl.ds(0, 6)], dst_ref=buf.at[e, s, pl.ds(0, 6)],
+            send_sem=send_sem.at[e], recv_sem=recv_sem.at[e, (s - 1) >> 1],
+            device_id=coords(partner(s)), device_id_type=MESH,
+        ).start()
+
+    def send_first(e):
+        for s in range(1, AHEAD + 1):
+            send_block(e, jnp.int32(s))
+
+    def wait_pair(e, m):
+        w = buf.at[e, pl.ds(2 * m + 1, 2), pl.ds(0, 6)]
+        pltpu.make_async_remote_copy(w, w, send_sem.at[e], recv_sem.at[e, m], device_id=coords(1), device_id_type=MESH).wait_recv()
 
     def send_params(first, count):
         @pl.loop(first, first + count)
@@ -108,6 +95,7 @@
 
     def velocity(e):
         own = blk[e]
+        buf[e, 0] = own
         own_parts = split3(own)
         parts = jnp.concatenate([p.astype(F32) for p in own_parts], axis=0).astype(BF16)
         row = lax.broadcasted_iota(jnp.int32, (24, 128), 0)
@@ -125,15 +113,19 @@
         near[...] = jnp.zeros_like(near)
 
         def expand(g):
-            h, m, l = [p.astype(F32) for p in split3(g)]
-            return jnp.concatenate([h, m, h, m, l, h], axis=0).astype(BF16), jnp.concatenate([h, m], axis=0).astype(BF16)
+            return [p.astype(F32) for p in split3(pack(g[0:3], g[3:6]))]
 
         def products(g, p):
-            prod[p] = dot(lhs[...], expand(g)[0], ((1,), (0,)))
+            h, m, l = expand(g)
+            prod[p] = dot(lhs[...], jnp.concatenate([h, m, h, m, l, h], axis=0).astype(BF16), ((1,), (0,)))
+
+        def two(g):
+            h, m, _ = expand(g)
+            return jnp.concatenate([h, m], axis=0).astype(BF16)
 
         def pair(g, p, both):
-            mine = expand(blk[e])[1]
-            theirs = expand(g)[1]
+            mine = two(blk[e])
+            theirs = two(g)
             high, low = [], []
             back = [[None] * 3 for _ in range(nodes // 128)]
             for r in range(0, nodes, ROWS):
@@ -174,7 +166,7 @@
         def give_back(s):
             k = partner(s)
 
-            @pl.when(k < half)
+            @pl.when((s > 0) & (s < half))
             def _():
                 pltpu.make_async_remote_copy(
                     src_ref=out.at[e, s], dst_ref=ret.at[e, k - 1],
@@ -182,35 +174,36 @@
                     device_id=coords(devices - k), device_id_type=MESH,
                 ).start()
 
-        wait_group(e, 0)
-        products(buf[e, 0], 0)
+        products(own, 0)
 
         @pl.loop(0, half // 2)
         def _(m):
             s = m * 2
 
-            @pl.when((lax.rem(m, GROUP // 2) == GROUP // 2 - 1) & (m < half // 2 - 1))
+            @pl.when(m < (half - AHEAD) // 2)
             def _():
-                wait_group(e, lax.div(s, GROUP) + 1)
+                send_block(e, AHEAD + 1 + s)
+                send_block(e, AHEAD + 2 + s)
+
+            if e is not STEPS:
+                @pl.when(e == 0)
+                def _():
+                    send_params(1 + m * 4, 4)
 
             @pl.when(m > 0)
             def _():
                 give_back(s - 2)
                 give_back(s - 1)
 
-            if e is not STEPS:
-                @pl.when(e == 0)
-                def _():
-                    send_params(1 + m * 4, 4)
-
-            products(buf[e, s + 1], 1)
-            out[e, s] = pair(buf[e, s], 0, True)
-            products(jnp.where(m < half // 2 - 1, buf[e, jnp.minimum(s + 2, half - 1)], blk[e]), 0)
-            out[e, s + 1] = pair(buf[e, s + 1], 1, True)
-
-        give_back(half - 2)
-        give_back(half - 1)
-        pair(blk[e], 0, False)
+            wait_pair(e, m)
+            products(buf[e, s + 1, 0:6], 1)
+            out[e, s] = pair(buf[e, s, 0:6], 0, True)
+            products(buf[e, s + 2, 0:6], 0)
+            out[e, s + 1] = pair(buf[e, s + 1, 0:6], 1, True)
+
+        give_back(jnp.int32(half - 2))
+        give_back(jnp.int32(half - 1))
+        pair(buf[e, half, 0:6], 0, False)
 
         ones = jnp.ones((8, 128), BF16)
         total = []
@@ -269,7 +262,7 @@
             out.append(surface + modulus[1:2] * (near - far - bend[c:c + 1]))
         return jnp.concatenate(out, axis=0)
 
-    send_block(0)
+    send_first(0)
     par_own[...] = par_ref[me]
 
     @pl.loop(0, STEPS)
@@ -282,12 +275,12 @@
             take_params()
 
         blk[e + 1] = pack(x, membrane(x))
-        send_block(e + 1)
+        send_first(e + 1)
 
     x_out[...] = blk[STEPS][0:3]
     v_out[...] = velocity(STEPS)
     for e in range(STEPS + 1):
-        w = buf.at[e]
+        w = buf.at[e, pl.ds(1, half), pl.ds(0, 6)]
         pltpu.make_async_remote_copy(w, w, send_sem.at[e], recv_sem.at[e, 0], device_id=coords(1), device_id_type=MESH).wait_send()
         w = ret.at[e, pl.ds(0, half - 1)]
         pltpu.make_async_remote_copy(w, w, ret_send.at[e], ret_recv.at[e], device_id=coords(1), device_id_type=MESH).wait_send()
@@ -313,7 +306,7 @@
             in_specs=[vmem] * 5,
             out_specs=(vmem, vmem),
             scratch_shapes=[
-                pltpu.VMEM((STEPS + 1, devices // 2, 8, nodes), F32),
+                pltpu.VMEM((STEPS + 1, devices // 2 + 1, 8, nodes), F32),
                 pltpu.VMEM((STEPS + 1, 8, nodes), F32),
                 pltpu.VMEM((STEPS + 1, devices // 2, 3, nodes), F32),
                 pltpu.VMEM((STEPS + 1, devices // 2, 3, nodes), F32),
@@ -326,7 +319,7 @@
                 pltpu.VMEM((3, nodes, 128), F32),
                 pltpu.VMEM((16, nodes), F32),
                 pltpu.SemaphoreType.DMA((STEPS + 1,)),
-                pltpu.SemaphoreType.DMA((STEPS + 1, devices // 2 // GROUP)),
+                pltpu.SemaphoreType.DMA((STEPS + 1, devices // 4)),
                 pltpu.SemaphoreType.DMA((STEPS + 1,)),
                 pltpu.SemaphoreType.DMA((STEPS + 1,)),
                 pltpu.SemaphoreType.DMA,

time: 152 us -> 144 us (0.947)
  Pallas kernels: 147 us -> 139 us
    pallas_call x1, Pallas kernels: 147 us -> 139 us  [body(): pl.pallas_call(functools.partial(kernel, n_src, devices, nodes, capacity,...]
where the time goes in v4:
time: 144 us
  Pallas kernels  139 us (97%)
  local copies, waits for them, and re-layouts  3.17 us (2%)
    pallas_call x1, Pallas kernels, body(): pl.pallas_call(functools.partial(kernel, n_src, devices, nodes, capacity,...  139 us

profile of v4, /device:TPU:1, one launch (start us, length us, event | category | flops | bytes accessed | tf_op | source)
XLA Modules:
  0.0 143.7 jit_solution(10000516030845739607)
XLA Ops:
  0.6 0.1 pad.8.clone
  0.7 0.9 maximum_maximum_fusion
  1.6 0.8 reshape.14
  2.4 0.3 copy.10
  2.7 0.1 copy.11
  2.8 0.0 copy-start
  2.8 0.0 copy-start.1
  2.9 0.0 copy-start.2
  2.9 0.0 copy-start.3
  2.9 0.6 copy-done
  3.6 0.0 copy-done.1
  3.6 0.0 copy-done.2
  3.6 0.0 copy-done.3
  3.6 138.9 %stokes.1 = (f32[3,256]{1,0:T(4,128)S(1)}, f32[3,256]{1,0:T(4,128)S(1)}) custom-call(f32[3,256]{1,0:T(4,128)S(1)} %copy-done.1, f32[3,256]{1,0:T(4,128)S(1)} %copy-done.2, s32[12,256]{1,0:T(8,128)S(1)} %copy-done, s32[1,256]{1,0:T(1,128)S(1)} %bitcast.5, f32[128,1,128]{2,1,0:T(1,128)S(1)} %pad.4.par_ref), custom_call_target="tpu_custom_call" | custom-call | tf_op jit(solution)/shard_map/stokes/pallas_call | solution.py:302
  142.5 0.6 copy.14
  143.1 0.6 copy.15
  (2 shorter events, 0.1 us)
Async XLA Ops:
  2.8 0.7 copy-start
  2.8 0.7 copy-start.1
  2.9 0.7 copy-start.2
  2.9 0.7 copy-start.3

commit v5 on v4

--- a/solution.py
+++ b/solution.py
@@ -11,10 +11,9 @@
 F32, BF16 = jnp.float32, jnp.bfloat16
 MESH = pl.DeviceIdType.MESH
 STEPS = 3
-EPS = 0.0025
+UNITS = 20.0
 TIME_STEP = 0.5
 ROWS = 16
-NEAR = 4
 AHEAD = 16
 FIELDS = 12
 
@@ -31,7 +30,7 @@
 
 
 def kernel(n_src, devices, nodes, capacity, scale, pos_ref, frc_ref, nbr_ref, own_ref, par_ref, x_out, v_out,
-           buf, blk, ret, out, par_buf, par_own, prm, xb, lhs, prod, acc, near, send_sem, recv_sem, ret_send, ret_recv, par_send, par_recv):
+           buf, blk, ret, out, par_buf, par_own, prm, place, xb, lhs, mine, theirs, prod, acc, near, send_sem, recv_sem, ret_send, ret_recv, par_send, par_recv):
     me = lax.axis_index("tgt") * n_src + lax.axis_index("src")
     half = devices // 2
 
@@ -57,14 +56,15 @@
     def pack(x, f):
         return jnp.concatenate([x, f, jnp.sum(x * f, axis=0, keepdims=True), jnp.ones((1, nodes), F32)], axis=0)
 
-    blk[0] = pack(pos_ref[...], frc_ref[...])
+    place[...] = pos_ref[...]
+    blk[0] = pack(pos_ref[...] * UNITS, frc_ref[...])
     pl.semaphore_wait(barrier, devices - 1)
 
     def partner(s):
-        t = s - NEAR - 1
-        far = 2 * NEAR + 1 + (t & 7) * ((half - 2 * NEAR) // 8) + (t >> 3)
-        near_by = jnp.where(s == half, half, s - half + 2 * NEAR + 1)
-        return jnp.where(s <= NEAR, s, jnp.where(s >= half - NEAR, near_by, far))
+        i, j = (s - 1) & 7, (s - 1) >> 3
+        turn = (i >> 1) + (i & 1) * (7 - 2 * (i >> 1))
+        last = half // 8 - 1
+        return jnp.where(j == last, 8 * (i + 1), 8 * turn + j + 1)
 
     def send_block(e, s):
         pltpu.make_async_remote_copy(
@@ -118,14 +118,12 @@
         def products(g, p):
             h, m, l = expand(g)
             prod[p] = dot(lhs[...], jnp.concatenate([h, m, h, m, l, h], axis=0).astype(BF16), ((1,), (0,)))
-
-        def two(g):
-            h, m, _ = expand(g)
-            return jnp.concatenate([h, m], axis=0).astype(BF16)
+            theirs[p] = jnp.concatenate([h, m], axis=0).astype(BF16)
+
+        h, m, _ = [p.astype(F32) for p in own_parts]
+        mine[...] = jnp.concatenate([h, m], axis=0).astype(BF16)
 
         def pair(g, p, both):
-            mine = two(blk[e])
-            theirs = two(g)
             high, low = [], []
             back = [[None] * 3 for _ in range(nodes // 128)]
             for r in range(0, nodes, ROWS):
@@ -135,10 +133,10 @@
                 for h in range(nodes // 128):
                     cols = slice(h * 128, (h + 1) * 128)
                     d = [xb[c, rows, :] - g[c:c + 1, cols] for c in range(3)]
-                    q = d[0] * d[0] + (d[1] * d[1] + (d[2] * d[2] + EPS))
+                    q = d[0] * d[0] + (d[1] * d[1] + (d[2] * d[2] + 1.0))
                     w = lax.rsqrt(q)
                     w3 = w * w * w
-                    direct = w + EPS * w3
+                    direct = w + w3
                     t = prod[p, rows, cols] * w3
                     for c in range(3):
                         total[c] = total[c] + t * d[c]
@@ -156,10 +154,10 @@
                 high.append(jnp.concatenate(highs, axis=1))
                 low.append(jnp.concatenate(lows, axis=1))
             high, low = jnp.concatenate(high, axis=0), jnp.concatenate(low, axis=0)
-            near[...] += dot(theirs, high, ((1,), (1,))) + dot(theirs, low, ((1,), (1,)))
+            near[...] += dot(theirs[p], high, ((1,), (1,))) + dot(theirs[p], low, ((1,), (1,)))
             if not both:
                 return None
-            rev = dot(mine, high, ((1,), (0,))) + dot(mine, low, ((1,), (0,)))
+            rev = dot(mine[...], high, ((1,), (0,))) + dot(mine[...], low, ((1,), (0,)))
             along = [jnp.concatenate([jnp.sum(b[c], axis=0, keepdims=True) for b in back], axis=1) for c in range(3)]
             return jnp.concatenate(along, axis=0) + rev[3:6] + rev[11:14]
 
@@ -213,7 +211,7 @@
         w = ret.at[e, pl.ds(0, half - 1)]
         pltpu.make_async_remote_copy(w, w, ret_send.at[e], ret_recv.at[e], device_id=coords(1), device_id_type=MESH).wait_recv()
         total = total + jnp.sum(ret[e, 0:half - 1], axis=0)
-        return total * scale
+        return total * (scale * UNITS)
 
     def take_params():
         w = par_buf.at[pl.ds(0, devices - 1)]
@@ -268,16 +266,17 @@
     @pl.loop(0, STEPS)
     def _(e):
         u = velocity(e)
-        x = blk[e][0:3] + TIME_STEP * u
+        x = place[...] + TIME_STEP * u
+        place[...] = x
 
         @pl.when(e == 0)
         def _():
             take_params()
 
-        blk[e + 1] = pack(x, membrane(x))
+        blk[e + 1] = pack(x * UNITS, membrane(x))
         send_first(e + 1)
 
-    x_out[...] = blk[STEPS][0:3]
+    x_out[...] = place[...]
     v_out[...] = velocity(STEPS)
     for e in range(STEPS + 1):
         w = buf.at[e, pl.ds(1, half), pl.ds(0, 6)]
@@ -313,8 +312,11 @@
                 pltpu.VMEM((devices, 1, 128), F32),
                 pltpu.VMEM((1, 128), F32),
                 pltpu.VMEM((16, nodes), F32),
+                pltpu.VMEM((3, nodes), F32),
                 pltpu.VMEM((3, nodes, 128), F32),
                 pltpu.VMEM((2 * nodes, 48), BF16),
+                pltpu.VMEM((16, nodes), BF16),
+                pltpu.VMEM((2, 16, nodes), BF16),
                 pltpu.VMEM((2, 2 * nodes, nodes), F32),
                 pltpu.VMEM((3, nodes, 128), F32),
                 pltpu.VMEM((16, nodes), F32),

time: 144 us -> 138 us (0.958)
  Pallas kernels: 139 us -> 133 us
    pallas_call x1, Pallas kernels: 139 us -> 133 us  [body(): pl.pallas_call(functools.partial(kernel, n_src, devices, nodes, capacity,...]
where the time goes in v5:
time: 138 us
  Pallas kernels  133 us (96%)
  local copies, waits for them, and re-layouts  3.17 us (2%)
    pallas_call x1, Pallas kernels, body(): pl.pallas_call(functools.partial(kernel, n_src, devices, nodes, capacity,...  133 us

profile of v5, /device:TPU:1, one launch (start us, length us, event | category | flops | bytes accessed | tf_op | source)
XLA Modules:
  0.0 137.6 jit_solution(2877794186593764719)
XLA Ops:
  0.6 0.1 pad.8.clone
  0.7 0.9 maximum_maximum_fusion
  1.6 0.8 reshape.14
  2.4 0.3 copy.10
  2.7 0.1 copy.11
  2.8 0.0 copy-start
  2.8 0.0 copy-start.1
  2.9 0.0 copy-start.2
  2.9 0.0 copy-start.3
  2.9 0.6 copy-done
  3.6 0.0 copy-done.1
  3.6 0.0 copy-done.2
  3.6 0.0 copy-done.3
  3.6 132.8 %stokes.1 = (f32[3,256]{1,0:T(4,128)S(1)}, f32[3,256]{1,0:T(4,128)S(1)}) custom-call(f32[3,256]{1,0:T(4,128)S(1)} %copy-done.1, f32[3,256]{1,0:T(4,128)S(1)} %copy-done.2, s32[12,256]{1,0:T(8,128)S(1)} %copy-done, s32[1,256]{1,0:T(1,128)S(1)} %bitcast.5, f32[128,1,128]{2,1,0:T(1,128)S(1)} %pad.4.par_ref), custom_call_target="tpu_custom_call" | custom-call | tf_op jit(solution)/shard_map/stokes/pallas_call | solution.py:301
  136.4 0.6 copy.14
  137.0 0.6 copy.15
  (2 shorter events, 0.1 us)
Async XLA Ops:
  2.8 0.7 copy-start
  2.8 0.7 copy-start.1
  2.9 0.7 copy-start.2
  2.9 0.7 copy-start.3

commit v6 on v5

--- a/solution.py
+++ b/solution.py
@@ -14,7 +14,7 @@
 UNITS = 20.0
 TIME_STEP = 0.5
 ROWS = 16
-AHEAD = 16
+AHEAD = 32
 FIELDS = 12
 
 
@@ -58,24 +58,27 @@
 
     place[...] = pos_ref[...]
     blk[0] = pack(pos_ref[...] * UNITS, frc_ref[...])
-    pl.semaphore_wait(barrier, devices - 1)
 
     def partner(s):
-        i, j = (s - 1) & 7, (s - 1) >> 3
-        turn = (i >> 1) + (i & 1) * (7 - 2 * (i >> 1))
-        last = half // 8 - 1
-        return jnp.where(j == last, 8 * (i + 1), 8 * turn + j + 1)
-
-    def send_block(e, s):
+        u = s - 3
+        i = u & 7
+        k = 8 * ((i >> 1) + (i & 1) * (7 - 2 * (i >> 1))) + (u >> 3) + 1
+        v = s - (half - 5)
+        step = 8 * ((v + 1) >> 1)
+        k = jnp.where(v >= 0, half // 2 + jnp.where((v & 1) == 1, -step, step), k)
+        k = jnp.where(s == half, half, k)
+        return jnp.where(s <= 2, jnp.where(s == 1, 8, half - 8), k)
+
+    def send_block(e, s, where):
         pltpu.make_async_remote_copy(
             src_ref=blk.at[e, pl.ds(0, 6)], dst_ref=buf.at[e, s, pl.ds(0, 6)],
             send_sem=send_sem.at[e], recv_sem=recv_sem.at[e, (s - 1) >> 1],
-            device_id=coords(partner(s)), device_id_type=MESH,
+            device_id=where, device_id_type=MESH,
         ).start()
 
     def send_first(e):
         for s in range(1, AHEAD + 1):
-            send_block(e, jnp.int32(s))
+            send_block(e, s, coords(partner(jnp.int32(s))))
 
     def wait_pair(e, m):
         w = buf.at[e, pl.ds(2 * m + 1, 2), pl.ds(0, 6)]
@@ -93,7 +96,15 @@
                     device_id=coords(k), device_id_type=MESH,
                 ).start()
 
-    def velocity(e):
+    def expand(g):
+        return [p.astype(F32) for p in split3(pack(g[0:3], g[3:6]))]
+
+    def products(g, p):
+        h, m, l = expand(g)
+        prod[p] = dot(lhs[...], jnp.concatenate([h, m, h, m, l, h], axis=0).astype(BF16), ((1,), (0,)))
+        theirs[p] = jnp.concatenate([h, m], axis=0).astype(BF16)
+
+    def prepare(e):
         own = blk[e]
         buf[e, 0] = own
         own_parts = split3(own)
@@ -112,17 +123,11 @@
         acc[...] = jnp.zeros_like(acc)
         near[...] = jnp.zeros_like(near)
 
-        def expand(g):
-            return [p.astype(F32) for p in split3(pack(g[0:3], g[3:6]))]
-
-        def products(g, p):
-            h, m, l = expand(g)
-            prod[p] = dot(lhs[...], jnp.concatenate([h, m, h, m, l, h], axis=0).astype(BF16), ((1,), (0,)))
-            theirs[p] = jnp.concatenate([h, m], axis=0).astype(BF16)
-
         h, m, _ = [p.astype(F32) for p in own_parts]
         mine[...] = jnp.concatenate([h, m], axis=0).astype(BF16)
-
+        products(own, 0)
+
+    def velocity(e):
         def pair(g, p, both):
             high, low = [], []
             back = [[None] * 3 for _ in range(nodes // 128)]
@@ -161,46 +166,51 @@
             along = [jnp.concatenate([jnp.sum(b[c], axis=0, keepdims=True) for b in back], axis=1) for c in range(3)]
             return jnp.concatenate(along, axis=0) + rev[3:6] + rev[11:14]
 
-        def give_back(s):
-            k = partner(s)
-
-            @pl.when((s > 0) & (s < half))
-            def _():
-                pltpu.make_async_remote_copy(
-                    src_ref=out.at[e, s], dst_ref=ret.at[e, k - 1],
-                    send_sem=ret_send.at[e], recv_sem=ret_recv.at[e],
-                    device_id=coords(devices - k), device_id_type=MESH,
-                ).start()
-
-        products(own, 0)
-
-        @pl.loop(0, half // 2)
-        def _(m):
+        def give_back(s, k, where):
+            pltpu.make_async_remote_copy(
+                src_ref=out.at[e, s], dst_ref=ret.at[e, k - 1],
+                send_sem=ret_send.at[e], recv_sem=ret_recv.at[e],
+                device_id=where, device_id_type=MESH,
+            ).start()
+
+        def targets(m):
+            s = m * 2
+            k1, k2 = partner(s - 2), partner(s - 1)
+            return (coords(partner(AHEAD + 1 + s)) + coords(partner(AHEAD + 2 + s))
+                    + (k1, k2) + coords(devices - k1) + coords(devices - k2))
+
+        def step(m, at):
             s = m * 2
 
             @pl.when(m < (half - AHEAD) // 2)
             def _():
-                send_block(e, AHEAD + 1 + s)
-                send_block(e, AHEAD + 2 + s)
+                send_block(e, AHEAD + 1 + s, at[0:2])
+                send_block(e, AHEAD + 2 + s, at[2:4])
 
             if e is not STEPS:
                 @pl.when(e == 0)
                 def _():
                     send_params(1 + m * 4, 4)
 
+            @pl.when(m > 1)
+            def _():
+                give_back(s - 2, at[4], at[6:8])
+
             @pl.when(m > 0)
             def _():
-                give_back(s - 2)
-                give_back(s - 1)
+                give_back(s - 1, at[5], at[8:10])
 
             wait_pair(e, m)
             products(buf[e, s + 1, 0:6], 1)
             out[e, s] = pair(buf[e, s, 0:6], 0, True)
             products(buf[e, s + 2, 0:6], 0)
             out[e, s + 1] = pair(buf[e, s + 1, 0:6], 1, True)
-
-        give_back(jnp.int32(half - 2))
-        give_back(jnp.int32(half - 1))
+            return targets(m + 1)
+
+        lax.fori_loop(0, half // 2, step, targets(jnp.int32(0)))
+        for s in (half - 2, half - 1):
+            k = partner(jnp.int32(s))
+            give_back(s, k, coords(devices - k))
         pair(buf[e, half, 0:6], 0, False)
 
         ones = jnp.ones((8, 128), BF16)
@@ -260,6 +270,8 @@
             out.append(surface + modulus[1:2] * (near - far - bend[c:c + 1]))
         return jnp.concatenate(out, axis=0)
 
+    prepare(0)
+    pl.semaphore_wait(barrier, devices - 1)
     send_first(0)
     par_own[...] = par_ref[me]
 
@@ -275,6 +287,7 @@
 
         blk[e + 1] = pack(x * UNITS, membrane(x))
         send_first(e + 1)
+        prepare(e + 1)
 
     x_out[...] = place[...]
     v_out[...] = velocity(STEPS)

time: 138 us -> 137 us (level)
  no operation moved by 1% of the time
where the time goes in v6:
time: 137 us
  Pallas kernels  132 us (96%)
  local copies, waits for them, and re-layouts  3.17 us (2%)
    pallas_call x1, Pallas kernels, body(): pl.pallas_call(functools.partial(kernel, n_src, devices, nodes, capacity,...  132 us

profile of v6, /device:TPU:1, one launch (start us, length us, event | category | flops | bytes accessed | tf_op | source)
XLA Modules:
  0.0 136.8 jit_solution(11599917823653701443)
XLA Ops:
  0.6 0.1 pad.8.clone
  0.7 0.9 maximum_maximum_fusion
  1.6 0.8 reshape.14
  2.4 0.3 copy.10
  2.7 0.1 copy.11
  2.8 0.0 copy-start
  2.8 0.0 copy-start.1
  2.9 0.0 copy-start.2
  2.9 0.0 copy-start.3
  2.9 0.6 copy-done
  3.6 0.0 copy-done.1
  3.6 0.0 copy-done.2
  3.6 0.0 copy-done.3
  3.6 132.1 %stokes.1 = (f32[3,256]{1,0:T(4,128)S(1)}, f32[3,256]{1,0:T(4,128)S(1)}) custom-call(f32[3,256]{1,0:T(4,128)S(1)} %copy-done.1, f32[3,256]{1,0:T(4,128)S(1)} %copy-done.2, s32[12,256]{1,0:T(8,128)S(1)} %copy-done, s32[1,256]{1,0:T(1,128)S(1)} %bitcast.5, f32[128,1,128]{2,1,0:T(1,128)S(1)} %pad.4.par_ref), custom_call_target="tpu_custom_call" | custom-call | tf_op jit(solution)/shard_map/stokes/pallas_call | solution.py:314
  135.6 0.6 copy.14
  136.2 0.6 copy.15
  (2 shorter events, 0.1 us)
Async XLA Ops:
  2.8 0.7 copy-start
  2.8 0.7 copy-start.1
  2.9 0.7 copy-start.2
  2.9 0.7 copy-start.3

commit v7 on v6

--- a/solution.py
+++ b/solution.py
@@ -14,7 +14,7 @@
 UNITS = 20.0
 TIME_STEP = 0.5
 ROWS = 16
-AHEAD = 32
+AHEAD = 24
 FIELDS = 12
 
 

time: 137 us -> 137 us (level)
  no operation moved by 1% of the time
where the time goes in v7:
time: 137 us; the launch traced here: 136 us
  Pallas kernels  132 us (96%)
  local copies, waits for them, and re-layouts  3.17 us (2%)
    pallas_call x1, Pallas kernels, body(): pl.pallas_call(functools.partial(kernel, n_src, devices, nodes, capacity,...  132 us

profile of v7, /device:TPU:1, one launch (start us, length us, event | category | flops | bytes accessed | tf_op | source)
XLA Modules:
  0.0 136.5 jit_solution(17966092651706663636)
XLA Ops:
  0.6 0.1 pad.8.clone
  0.7 0.9 maximum_maximum_fusion
  1.6 0.8 reshape.14
  2.4 0.3 copy.10
  2.7 0.1 copy.11
  2.8 0.0 copy-start
  2.8 0.0 copy-start.1
  2.9 0.0 copy-start.2
  2.9 0.0 copy-start.3
  2.9 0.6 copy-done
  3.6 0.0 copy-done.1
  3.6 0.0 copy-done.2
  3.6 0.0 copy-done.3
  3.6 131.7 %stokes.1 = (f32[3,256]{1,0:T(4,128)S(1)}, f32[3,256]{1,0:T(4,128)S(1)}) custom-call(f32[3,256]{1,0:T(4,128)S(1)} %copy-done.1, f32[3,256]{1,0:T(4,128)S(1)} %copy-done.2, s32[12,256]{1,0:T(8,128)S(1)} %copy-done, s32[1,256]{1,0:T(1,128)S(1)} %bitcast.5, f32[128,1,128]{2,1,0:T(1,128)S(1)} %pad.4.par_ref), custom_call_target="tpu_custom_call" | custom-call | tf_op jit(solution)/shard_map/stokes/pallas_call | solution.py:314
  135.3 0.6 copy.14
  135.9 0.6 copy.15
  (2 shorter events, 0.1 us)
Async XLA Ops:
  2.8 0.7 copy-start
  2.8 0.7 copy-start.1
  2.9 0.7 copy-start.2
  2.9 0.7 copy-start.3
